TPU v7x, 256 devices: a whole 4x4x8 slice. The times are simulated.
256 devices in a mesh: list: 32 (over x, y, core), rep: 8 (over z).
Axes of the slice: x: 4, y: 4, z: 8, core: 2. Of those that a mesh axis runs over, the one named last changes fastest.
Arguments:
- memory_rows: bfloat16 [65536, 1024], P(('list', 'rep'))
- list_owner: int32 [65536, 1], P(('list', 'rep')), may hold values from 0 to 31; in each aligned block of 256 rows (0 to 255, 256 to 511, ...) at most 32 rows name the same one
- list_slot: int32 [65536], P(('list', 'rep')), may hold values from 0 to 2047
- pq_codes: int32 [65536, 16], P(('list', 'rep')), may hold values from 0 to 255
- valid_rows: int32 [256], P(('list', 'rep')), may hold values from 128 to 256
- centroids: bfloat16 [65536, 1024], P('list'), may hold values from -3 to 3
- codebook: float32 [16, 256, 64], replicated
Outputs:
- new_codebook: float32 [16, 256, 64], P('rep')
- row_error: float32 [65536], P(('list', 'rep'))
Inputs may be any that keep to these rules, and one draw needn't show every extreme that they name: `list_owner`: the rows of one device name one index of list at most 32 times, and some device's rows name one exactly 32 times.
All inputs are finite; a program needn't handle non-finite values.
Results may differ from a plain program's by a relative error of at most 0.0038.
Values may be sent and summed in bfloat16 or wider, within the bound.
A program may use at most 128 MiB of HBM per device.

v0:
```python
import jax
import jax.numpy as jnp
from jax import lax
from jax.sharding import PartitionSpec as P

prior_weight = 4.0


def code_statistics(residual, pq_codes, is_live, codebook):
    row_count = residual.shape[0]
    subspaces = codebook.shape[0]
    code_count = codebook.shape[1]
    width_sub = codebook.shape[2]
    residual = jnp.where(is_live[:, None], residual, 0.0)
    recon = codebook[jnp.arange(subspaces)[None, :], pq_codes].reshape(
        row_count, subspaces * width_sub
    )
    row_error = jnp.where(is_live, jnp.mean((residual - recon) ** 2, axis=1), 0.0)
    rounded = (
        residual.astype(jnp.bfloat16).reshape(row_count, subspaces, width_sub).transpose(1, 0, 2)
    )
    codes_major = pq_codes.T

    def per_subspace(item):
        code_col, part_rows = item
        onehot = ((code_col[:, None] == jnp.arange(code_count)[None, :]) & is_live[:, None]).astype(
            jnp.bfloat16
        )
        sums_one = lax.dot_general(
            onehot, part_rows, (((0,), (0,)), ((), ())), preferred_element_type=jnp.float32
        )
        counts_one = jnp.sum(onehot.astype(jnp.float32), axis=0)
        return (sums_one, counts_one)

    sums, counts = lax.map(per_subspace, (codes_major, rounded))
    return (row_error, sums, counts)


def body(memory_rows, list_owner, list_slot, pq_codes, valid_rows, centroids, codebook):
    row_count = memory_rows.shape[0]
    width = memory_rows.shape[1]
    list_count = centroids.shape[0]
    owners = lax.axis_size("list")
    capacity = 4 * row_count // owners
    is_valid = jnp.arange(row_count) < valid_rows[0]
    target = list_owner[:, 0]
    onehot_dest = ((target[:, None] == jnp.arange(owners)[None, :]) & is_valid[:, None]).astype(
        jnp.int32
    )
    before = jnp.cumsum(onehot_dest, axis=0) - onehot_dest
    slot_rank = jnp.sum(before * onehot_dest, axis=1)
    position = jnp.where(is_valid, target * capacity + slot_rank, owners * capacity)
    taken = jnp.clip(position, 0, owners * capacity - 1)
    total_slots = owners * capacity
    send_rows = (
        jnp.zeros((total_slots, width), jnp.bfloat16).at[position].set(memory_rows, mode="drop")
    )
    send_slot = jnp.full((total_slots,), -1, jnp.int32).at[position].set(list_slot, mode="drop")
    send_codes = (
        jnp.zeros((total_slots, pq_codes.shape[1]), jnp.int32)
        .at[position]
        .set(pq_codes, mode="drop")
    )
    got_rows, got_slot, got_codes = (
        lax.all_to_all(
            send_rows.reshape(owners, capacity, width),
            "list",
            split_axis=0,
            concat_axis=0,
            tiled=True,
        ),
        lax.all_to_all(
            send_slot.reshape(owners, capacity), "list", split_axis=0, concat_axis=0, tiled=True
        ),
        lax.all_to_all(
            send_codes.reshape(owners, capacity, pq_codes.shape[1]),
            "list",
            split_axis=0,
            concat_axis=0,
            tiled=True,
        ),
    )
    got_rows = got_rows.reshape(total_slots, width)
    got_slot = got_slot.reshape(total_slots)
    got_codes = got_codes.reshape(total_slots, pq_codes.shape[1])
    is_live = got_slot >= 0
    centre = centroids[jnp.clip(got_slot, 0, list_count - 1)].astype(jnp.float32)
    residual = got_rows.astype(jnp.float32) - centre
    slot_error, sums, counts = code_statistics(residual, got_codes, is_live, codebook)
    returned = lax.all_to_all(
        slot_error.reshape(owners, capacity), "list", split_axis=0, concat_axis=0, tiled=True
    )
    row_error = jnp.where(is_valid, returned.reshape(total_slots)[taken], 0.0)
    subspaces = codebook.shape[0]
    replicas = lax.axis_size("rep")
    share = subspaces // replicas
    first_sub = lax.axis_index("rep") * share
    sums_all, counts_all = lax.psum((sums, counts), ("list", "rep"))
    sums_mine = lax.dynamic_slice_in_dim(sums_all, first_sub, share, 0)
    counts_mine = lax.dynamic_slice_in_dim(counts_all, first_sub, share, 0)
    old_mine = lax.dynamic_slice_in_dim(codebook, first_sub, share, 0)
    new_codebook = (sums_mine + prior_weight * old_mine) / (counts_mine[:, :, None] + prior_weight)
    return (new_codebook, row_error)


def solution(mesh):
    in_specs = (
        P(("list", "rep"), None),
        P(("list", "rep"), None),
        P(("list", "rep")),
        P(("list", "rep"), None),
        P(("list", "rep")),
        P("list", None),
        P(),
    )
    out_specs = (P("rep", None, None), P(("list", "rep")))
    return jax.shard_map(body, mesh=mesh, in_specs=in_specs, out_specs=out_specs, check_vma=False)
```

profile of v0, /device:TPU:2, one launch (start us, length us, event | category | flops | bytes accessed | tf_op | source)
XLA Modules:
  0.0 582.1 jit_solution(2420515403371690203)
XLA Ops:
  7.8 0.7 fusion.22
  9.3 0.9 fusion.19
  10.2 0.7 compare_select_fusion.2
  10.9 1.6 scatter_custom_fusion.1
  12.5 0.7 all_to_all.17
  13.1 7.6 %all-to-all-start.1 = ((s32[32,1,32]{2,1,0:T(1,128)}), s32[32,1,32]{2,1,0:T(1,128)S(1)}, u32[]{:S(2)}, u32[]{:S(2)}) async-start(s32[32,1,32]{2,1,0:T(1,128)} %all_to_all.17), calls=%async_computation.1 | async-start | bytes 32768 | tf_op jit(solution)/shard_map/all_to_all | solution.py:72
  20.8 0.8 copy.39
  21.6 1.3 scatter_custom_fusion
  23.1 0.8 reshape.243
  23.9 3.1 all-to-all-done.1
  26.9 5.0 all-to-all-start
  31.9 3.7 scatter_custom_fusion.2
  35.6 2.7 all-to-all-done
  38.3 5.8 %all-to-all-start.2 = ((bf16[32,32,1024]{2,1,0:T(8,128)(2,1)}), bf16[32,32,1024]{2,1,0:T(8,128)(2,1)}, u32[]{:S(2)}, u32[]{:S(2)}) async-start(bf16[32,32,1024]{2,1,0:T(8,128)(2,1)} %bitcast.13), calls=%async_computation.2 | async-start | bytes 4194304 | tf_op jit(solution)/shard_map/all_to_all | solution.py:65
  45.2 8.8 %gather_fusion = bf16[1024,1024]{1,0:T(8,128)(2,1)} fusion(bf16[2048,1024]{1,0:T(8,128)(2,1)} %param.14, s32[1024]{0:T(1024)S(1)} %broadcast_clamp_fusion.1), kind=kCustom, calls=%fused_computation | custom fusion | bytes 4198400 | tf_op jit(solution)/shard_map/gather | solution.py:87
  53.9 4.1 copy.44
  58.0 4.0 convert_element_type.53
  62.0 8.1 %copy.45 = f32[1024,16,64]{2,1,0:T(8,128)} copy(f32[1024,16,64]{0,2,1:T(8,128)} %bitcast.73) | data formatting | bytes 8388608 | tf_op jit(solution)/shard_map/convert_element_type | solution.py:87
  70.7 0.8 reduce.8
  72.4 176.0 %gather_fusion.1 = f32[16384,64]{1,0:T(8,128)} fusion(f32[16,256,64]{2,1,0:T(8,128)S(1)} %copy.49, s32[16384]{0:T(1024)S(1)} %reshape.188), kind=kCustom, calls=%fused_computation.1 | custom fusion | bytes 8519680 | tf_op jit(solution)/shard_map/gather | solution.py:15
  248.5 7.6 %gather.13 = f32[32,32,1024]{2,1,0:T(8,128)} reshape(f32[16384,64]{1,0:T(8,128)} %gather_fusion.1) | data formatting | bytes 8388608 | tf_op jit(solution)/shard_map/gather | solution.py:15
  256.1 6.9 %reshape.177 = f32[1024,16,64]{2,1,0:T(8,128)} reshape(bf16[32,32,1024]{2,1,0:T(8,128)(2,1)} %all-to-all-done.2) | data formatting | bytes 6291456 | tf_op jit(solution)/shard_map/convert_element_type | solution.py:88
  262.9 7.7 %fusion.9 = bf16[16,1024,64]{2,0,1:T(8,128)(2,1)S(1)} fusion(f32[1024,16,64]{2,1,0:T(8,128)} %reshape.177, f32[1024,16,64]{2,1,0:T(8,128)} %copy.45, pred[1024]{0:T(1024)(128)(4,1)S(1)} %ge.17), kind=kLoop, calls=%fused_computation.19 | loop fusion | flops 3145728 | bytes 10486784 | tf_op jit(solution)/shard_map/transpose | solution.py:20
  270.6 3.0 copy.46
  273.6 40.9 %while.12 = (s32[]{:T(128)}, f32[16,256,64]{1,2,0:T(8,128)}, f32[16,256]{1,0:T(8,128)S(1)}, s32[16,1024]{1,0:T(8,128)S(1)}, pred[1024]{0:T(1024)(128)(4,1)S(1)},...) while((s32[]{:T(128)}, f32[16,256,64]{1,2,0:T(8,128)}, f32[16,256]{1,0:T(8,128)S(1)}, ...), condition=%wide.region_8.9_spmd, body=%wide.region_6.8_spmd.sunk | while | flops 35389184 | bytes 350301 | solution.py:35
  273.6 2.1 fusion.31
  276.2 2.1 fusion.31
  278.8 2.1 fusion.31
  281.3 2.1 fusion.31
  283.9 2.1 fusion.31
  286.4 2.1 fusion.31
  289.0 2.1 fusion.31
  291.5 2.1 fusion.31
  294.1 2.1 fusion.31
  296.6 2.1 fusion.31
  299.2 2.1 fusion.31
  301.8 2.1 fusion.31
  304.3 2.1 fusion.31
  306.9 2.1 fusion.31
  309.4 2.1 fusion.31
  312.0 2.1 fusion.31
  314.6 5.1 multiply_reduce_fusion
  320.3 7.4 %all-to-all-start.3 = ((f32[32,1,32]{2,1,0:T(1,128)}), f32[32,1,32]{2,1,0:T(1,128)S(1)}, u32[]{:S(2)}, u32[]{:S(2)}) async-start(f32[32,1,32]{2,1,0:T(1,128)} %bitcast.21), calls=%async_computation.3 | async-start | bytes 32768 | tf_op jit(solution)/shard_map/all_to_all | solution.py:90
  327.7 79.8 %psum.15 = f32[16,256]{1,0:T(8,128)S(1)} all-reduce(f32[16,256]{1,0:T(8,128)S(1)} %get-tuple-element.36), channel_id=1, replica_groups=mesh['list'=32,'rep'=8] {'list','rep'}, use_global_device_ids=true, to_apply=%region_10.11 | all-reduce | flops 4096 | bytes 32768 | tf_op jit(solution)/shard_map/psum | solution.py:98
  408.0 0.7 reduce.7
  408.8 1.4 gather_fusion.2
  410.7 162.9 %all-reduce.2.cloned.1.call-done = f32[16,256,64]{1,2,0:T(8,128)} async-done(((f32[16,256,64]{1,2,0:T(8,128)}), f32[16,256,64]{1,2,0:T(8,128)}) %all-reduce.2.cloned.1.call-update) | async-done | bytes 1048592 | tf_op jit(solution)/shard_map/psum | solution.py:98
  573.6 1.6 add_divide_fusion
  (86 shorter events, 11.6 us)
Async XLA Ops:
  9.1 35.3 %copy-start = (f32[16,256,64]{1,2,0:T(8,128)S(1)}, f32[16,256,64]{1,2,0:T(8,128)}, u32[]{:S(2)}) copy-start(f32[16,256,64]{1,2,0:T(8,128)} %param.15) | copy-start | bytes 3145732
  13.1 13.8 %all-to-all-start.1 = ((s32[32,1,32]{2,1,0:T(1,128)}), s32[32,1,32]{2,1,0:T(1,128)S(1)}, u32[]{:S(2)}, u32[]{:S(2)}) async-start(s32[32,1,32]{2,1,0:T(1,128)} %all_to_all.17), calls=%async_computation.1 | async-start | bytes 32768 | tf_op jit(solution)/shard_map/all_to_all | solution.py:72
  26.9 11.4 %all-to-all-start = ((s32[32,1,512]{2,1,0:T(1,128)}), s32[32,1,512]{2,1,0:T(1,128)S(1)}, u32[]{:S(2)}, u32[]{:S(2)}) async-start(s32[32,1,512]{2,1,0:T(1,128)} %reshape.243), calls=%async_computation | async-start | bytes 131072 | tf_op jit(solution)/shard_map/all_to_all | solution.py:75
  38.3 217.7 %all-to-all-start.2 = ((bf16[32,32,1024]{2,1,0:T(8,128)(2,1)}), bf16[32,32,1024]{2,1,0:T(8,128)(2,1)}, u32[]{:S(2)}, u32[]{:S(2)}) async-start(bf16[32,32,1024]{2,1,0:T(8,128)(2,1)} %bitcast.13), calls=%async_computation.2 | async-start | bytes 4194304 | tf_op jit(solution)/shard_map/all_to_all | solution.py:65
  44.2 529.5 %all-reduce.2.cloned.1.call-start = ((), (), s32[]{:S(2)}) async-start(), calls=%async_computation.4 | async-start | bytes 2097152 | tf_op jit(solution)/shard_map/psum | solution.py:98
  320.3 87.2 %all-to-all-start.3 = ((f32[32,1,32]{2,1,0:T(1,128)}), f32[32,1,32]{2,1,0:T(1,128)S(1)}, u32[]{:S(2)}, u32[]{:S(2)}) async-start(f32[32,1,32]{2,1,0:T(1,128)} %bitcast.21), calls=%async_computation.3 | async-start | bytes 32768 | tf_op jit(solution)/shard_map/all_to_all | solution.py:90
Sparse Core Ops, SparseCore 0:
  314.7 258.9 all-reduce.1
where the time goes:
time: 584 us; the launch traced here: 582 us
  local copies, waits for them, and re-layouts  229 us (39%)
  waiting for transfers between devices  169 us (29%)
  blocking collectives  79.8 us (14%)
  matrix products  34 us (6%)
  other arithmetic  29.6 us (5%)
  starting transfers between devices  26.1 us (4%)
  between operations  14.9 us (3%)
    gather x2, local copies, waits for them, and re-layouts, code_statistics(): codebook[jnp.arange(subspaces)[None, :], pq_codes]  184 us
    psum x1, waiting for transfers between devices, body(): sums_all, counts_all = lax.psum((sums, counts), ('list', 'rep'))  163 us
    psum x1, blocking collectives, body(): sums_all, counts_all = lax.psum((sums, counts), ('list', 'rep'))  79.8 us
    dot_general x16, matrix products, per_subspace(): lax.dot_general(onehot, part_rows, (((0,), (0,)), ((), ())), preferred_el...  34 us
    convert_element_type x2, local copies, waits for them, and re-layouts, body(): centroids[jnp.clip(got_slot, 0, list_count - 1)].astype(jnp.float32)  12.2 us
  transfers between devices with their start and end apart: 5, of which 3 were waited for; matrix products, arithmetic and copies ran while one was open for 39% of the time, Pallas kernels for 0%

commit v1 on v0

--- a/solution.py
+++ b/solution.py
@@ -95,7 +95,7 @@
     replicas = lax.axis_size("rep")
     share = subspaces // replicas
     first_sub = lax.axis_index("rep") * share
-    sums_all, counts_all = lax.psum((sums, counts), ("list", "rep"))
+    sums_all, counts_all = lax.psum(lax.psum((sums, counts), axis_name="list"), axis_name="rep")
     sums_mine = lax.dynamic_slice_in_dim(sums_all, first_sub, share, 0)
     counts_mine = lax.dynamic_slice_in_dim(counts_all, first_sub, share, 0)
     old_mine = lax.dynamic_slice_in_dim(codebook, first_sub, share, 0)

time: 584 us -> 502 us (0.86)
  the two profiles are of different devices: /device:TPU:2 before, /device:TPU:0 now
where the time goes in v1:
time: 502 us; the launch traced here: 501 us
  local copies, waits for them, and re-layouts  229 us (46%)
  blocking collectives  161 us (32%)
  matrix products  34 us (7%)
  other arithmetic  29.7 us (6%)
  starting transfers between devices  18.3 us (4%)
  between operations  14.9 us (3%)
  waiting for transfers between devices  13.2 us (3%)
    gather x2, local copies, waits for them, and re-layouts, code_statistics(): codebook[jnp.arange(subspaces)[None, :], pq_codes]  184 us
    psum x1, blocking collectives, body(): lax.psum((sums, counts), axis_name='list')  129 us
    dot_general x16, matrix products, per_subspace(): lax.dot_general(onehot, part_rows, (((0,), (0,)), ((), ())), preferred_el...  34 us
    psum x1, blocking collectives, body(): lax.psum(lax.psum((sums, counts), axis_name='list'), axis_name='rep')  32.7 us
    convert_element_type x2, local copies, waits for them, and re-layouts, body(): centroids[jnp.clip(got_slot, 0, list_count - 1)].astype(jnp.float32)  12.2 us
  transfers between devices with their start and end apart: 6, of which 3 were waited for; matrix products, arithmetic and copies ran while one was open for 45% of the time, Pallas kernels for 0%

profile of v1, /device:TPU:0, one launch (start us, length us, event | category | flops | bytes accessed | tf_op | source)
XLA Modules:
  0.0 500.6 jit_solution(5048934553795387928)
XLA Ops:
  7.8 0.7 fusion.22
  9.3 0.9 fusion.19
  10.2 0.7 compare_select_fusion.2
  10.9 1.6 scatter_custom_fusion.1
  13.1 5.6 %all-to-all-start.1 = ((s32[32,1,32]{2,1,0:T(1,128)}), s32[32,1,32]{2,1,0:T(1,128)S(1)}, u32[]{:S(2)}, u32[]{:S(2)}) async-start(s32[32,1,32]{2,1,0:T(1,128)} %all_to_all.17), calls=%async_computation.1 | async-start | bytes 32768 | tf_op jit(solution)/shard_map/all_to_all | solution.py:72
  18.7 0.8 copy.39
  19.5 1.3 scatter_custom_fusion
  21.0 0.8 reshape.243
  21.8 4.3 all-to-all-done.1
  26.1 3.9 all-to-all-start
  30.0 3.8 scatter_custom_fusion.2
  33.7 3.7 all-to-all-done
  37.5 4.8 all-to-all-start.2
  43.2 8.8 %gather_fusion = bf16[1024,1024]{1,0:T(8,128)(2,1)} fusion(bf16[2048,1024]{1,0:T(8,128)(2,1)} %param.14, s32[1024]{0:T(1024)S(1)} %broadcast_clamp_fusion.1), kind=kCustom, calls=%fused_computation | custom fusion | bytes 4198400 | tf_op jit(solution)/shard_map/gather | solution.py:87
  52.0 4.1 copy.44
  56.1 8.1 %copy.45 = f32[1024,16,64]{2,1,0:T(8,128)} copy(f32[1024,16,64]{0,2,1:T(8,128)} %bitcast.73) | data formatting | bytes 8388608 | tf_op jit(solution)/shard_map/convert_element_type | solution.py:87
  64.8 0.8 reduce.8
  66.0 5.1 %all-to-all-done.2 = bf16[32,32,1024]{2,1,0:T(8,128)(2,1)} async-done(((bf16[32,32,1024]{2,1,0:T(8,128)(2,1)}), bf16[32,32,1024]{2,1,0:T(8,128)(2,1)}, u32[]{:S(2)}, u32[]{:S(2)}) %all-to-all-start.2) | async-done | bytes 2097184 | tf_op jit(solution)/shard_map/all_to_all | solution.py:65
  71.1 6.9 %reshape.177 = f32[1024,16,64]{2,1,0:T(8,128)} reshape(bf16[32,32,1024]{2,1,0:T(8,128)(2,1)} %all-to-all-done.2) | data formatting | bytes 6291456 | tf_op jit(solution)/shard_map/convert_element_type | solution.py:88
  78.0 7.7 %fusion.9 = bf16[16,1024,64]{2,0,1:T(8,128)(2,1)S(1)} fusion(f32[1024,16,64]{2,1,0:T(8,128)} %reshape.177, f32[1024,16,64]{2,1,0:T(8,128)} %copy.45, pred[1024]{0:T(1024)(128)(4,1)S(1)} %ge.17), kind=kLoop, calls=%fused_computation.19 | loop fusion | flops 3145728 | bytes 10486784 | tf_op jit(solution)/shard_map/transpose | solution.py:20
  85.7 3.0 copy.46
  88.7 40.9 %while.12 = (s32[]{:T(128)}, f32[16,256,64]{1,2,0:T(8,128)}, f32[16,256]{1,0:T(8,128)S(1)}, s32[16,1024]{1,0:T(8,128)S(1)}, pred[1024]{0:T(1024)(128)(4,1)S(1)},...) while((s32[]{:T(128)}, f32[16,256,64]{1,2,0:T(8,128)}, f32[16,256]{1,0:T(8,128)S(1)}, ...), condition=%wide.region_8.9_spmd, body=%wide.region_6.8_spmd.sunk | while | flops 35389184 | bytes 350301 | solution.py:35
  88.7 2.1 fusion.31
  91.2 2.1 fusion.31
  93.8 2.1 fusion.31
  96.4 2.1 fusion.31
  98.9 2.1 fusion.31
  101.5 2.1 fusion.31
  104.0 2.1 fusion.31
  106.6 2.1 fusion.31
  109.1 2.1 fusion.31
  111.7 2.1 fusion.31
  114.2 2.1 fusion.31
  116.8 2.1 fusion.31
  119.4 2.1 fusion.31
  121.9 2.1 fusion.31
  124.5 2.1 fusion.31
  127.0 2.1 fusion.31
  129.6 4.0 convert_element_type.53
  134.2 176.0 %gather_fusion.1 = f32[16384,64]{1,0:T(8,128)} fusion(f32[16,256,64]{2,1,0:T(8,128)S(1)} %copy.49, s32[16384]{0:T(1024)S(1)} %reshape.188), kind=kCustom, calls=%fused_computation.1 | custom fusion | bytes 8519680 | tf_op jit(solution)/shard_map/gather | solution.py:15
  310.3 7.6 %gather.13 = f32[32,32,1024]{2,1,0:T(8,128)} reshape(f32[16384,64]{1,0:T(8,128)} %gather_fusion.1) | data formatting | bytes 8388608 | tf_op jit(solution)/shard_map/gather | solution.py:15
  317.9 5.1 %multiply_reduce_fusion = f32[32,32]{1,0:T(8,128)S(1)} fusion(f32[32,32,1024]{2,1,0:T(8,128)} %gather.13, f32[32,32,1024]{2,1,0:T(8,128)} %bitcast.74, pred[32,32]{1,0:T(8,128)(4,1)S(1)} %fusion.25, bf16[32,32,1024]{2,1,0:T(8,128)(2,1)} %all-to-all-done.2), kind=kLoop, calls=%fused_computation.20 | loop fusion | flops 6290432 | bytes 10490880 | tf_op jit(solution)/shard_map/reduce_sum | solution.py:18
  323.6 3.8 all-to-all-start.3
  327.5 128.7 %psum.30 = f32[16,256]{1,0:T(8,128)S(1)} all-reduce(f32[16,256]{1,0:T(8,128)S(1)} %get-tuple-element.36), channel_id=1, replica_groups=mesh['list'=32,'rep'=8] {'list'}, use_global_device_ids=true, to_apply=%region_11.12 | all-reduce | flops 4096 | bytes 32768 | tf_op jit(solution)/shard_map/psum | solution.py:98
  456.1 32.7 %psum.31 = f32[16,256]{1,0:T(8,128)S(1)} all-reduce(f32[16,256]{1,0:T(8,128)S(1)} %psum.30), channel_id=1, replica_groups=mesh['list'=32,'rep'=8] {'rep'}, use_global_device_ids=true, to_apply=%region_12.13 | all-reduce | flops 4096 | bytes 32768 | tf_op jit(solution)/shard_map/psum | solution.py:98
  489.4 0.7 reduce.7
  490.2 1.4 gather_fusion.2
  492.1 1.6 add_divide_fusion
  (90 shorter events, 12.4 us)
Async XLA Ops:
  9.1 33.4 %copy-start = (f32[16,256,64]{1,2,0:T(8,128)S(1)}, f32[16,256,64]{1,2,0:T(8,128)}, u32[]{:S(2)}) copy-start(f32[16,256,64]{1,2,0:T(8,128)} %param.15) | copy-start | bytes 3145732
  13.1 13.0 %all-to-all-start.1 = ((s32[32,1,32]{2,1,0:T(1,128)}), s32[32,1,32]{2,1,0:T(1,128)S(1)}, u32[]{:S(2)}, u32[]{:S(2)}) async-start(s32[32,1,32]{2,1,0:T(1,128)} %all_to_all.17), calls=%async_computation.1 | async-start | bytes 32768 | tf_op jit(solution)/shard_map/all_to_all | solution.py:72
  26.1 11.4 %all-to-all-start = ((s32[32,1,512]{2,1,0:T(1,128)}), s32[32,1,512]{2,1,0:T(1,128)S(1)}, u32[]{:S(2)}, u32[]{:S(2)}) async-start(s32[32,1,512]{2,1,0:T(1,128)} %reshape.243), calls=%async_computation | async-start | bytes 131072 | tf_op jit(solution)/shard_map/all_to_all | solution.py:75
  37.5 33.6 %all-to-all-start.2 = ((bf16[32,32,1024]{2,1,0:T(8,128)(2,1)}), bf16[32,32,1024]{2,1,0:T(8,128)(2,1)}, u32[]{:S(2)}, u32[]{:S(2)}) async-start(bf16[32,32,1024]{2,1,0:T(8,128)(2,1)} %bitcast.13), calls=%async_computation.2 | async-start | bytes 4194304 | tf_op jit(solution)/shard_map/all_to_all | solution.py:65
  42.3 275.6 %all-reduce.3.cloned.1.call-start = ((), (), s32[]{:S(2)}) async-start(), calls=%async_computation.4 | async-start | bytes 2097152 | tf_op jit(solution)/shard_map/psum | solution.py:98
  129.6 362.5 %all-reduce.5.cloned.1.call-start = ((), (), s32[]{:S(2)}) async-start(), calls=%async_computation.5 | async-start | bytes 2097152 | tf_op jit(solution)/shard_map/psum | solution.py:98
  323.6 165.3 %all-to-all-start.3 = ((f32[32,1,32]{2,1,0:T(1,128)}), f32[32,1,32]{2,1,0:T(1,128)S(1)}, u32[]{:S(2)}, u32[]{:S(2)}) async-start(f32[32,1,32]{2,1,0:T(1,128)} %bitcast.21), calls=%async_computation.3 | async-start | bytes 32768 | tf_op jit(solution)/shard_map/all_to_all | solution.py:90
Sparse Core Ops, SparseCore 0:
  129.7 113.7 all-reduce.2
  318.0 75.0 all-reduce.4
